TPU v7x, 32 devices: a whole 2x2x4 slice. The times are simulated.
32 devices in a mesh: groups: 2 (over x), seq: 8 (over z, y), head: 2 (over core).
Axes of the slice: x: 2, y: 2, z: 4, core: 2. Of those that a mesh axis runs over, the one named last changes fastest.
Arguments:
- query_proj: bfloat16 [4096, 2048], P(('groups', 'seq'), 'head'), parts along dimension 0, may hold values from -6 to 6
- key_proj: bfloat16 [4096, 2048], P(('groups', 'seq'), 'head'), parts along dimension 0, may hold values from -6 to 6
- value_proj: bfloat16 [4096, 2048], P(('groups', 'seq'), 'head'), parts along dimension 0, may hold values from -6 to 6
- segment_ids: int32 [4096], P(('groups', 'seq')), parts along dimension 0, may hold values from 0 to 5, never falling along the last dimension, each value on 1 to 682 neighbouring positions
- feature_map: bfloat16 [16, 128, 256], P('head'), may hold values from -0.5 to 0.5
- head_gain: float32 [2048], P('head'), may hold values from 0.1 to 1.9
- residual: bfloat16 [4096, 2048], P(('groups', 'seq', 'head')), parts along dimension 0, may hold values from -6 to 6
- out_weight: bfloat16 [2048, 2048], P('head'), may hold values from -0.125 to 0.125
- norm_gain: float32 [2048], replicated, may hold values from 0.1 to 1.9
- router: bfloat16 [2048, 16], replicated, may hold values from -0.125 to 0.125
- w_gate: bfloat16 [16, 2048, 1024], P(('seq', 'head')), may hold values from -0.125 to 0.125
- w_up: bfloat16 [16, 2048, 1024], P(('seq', 'head')), may hold values from -0.125 to 0.125
- w_down: bfloat16 [16, 1024, 2048], P(('seq', 'head')), may hold values from -0.1875 to 0.1875
- expert_ids: int32 [4096, 8], P(('groups', 'seq', 'head')), parts along dimension 0, may hold values from 0 to 15, all different within a row; in each aligned block of 128 rows (0 to 127, 128 to 255, ...) at most 80 rows name the same one
Outputs:
- hidden: bfloat16 [4096, 2048], P(('groups', 'seq', 'head')), parts along dimension 0
- expert_sum: bfloat16 [4096, 2048], P(('groups', 'seq', 'head')), parts along dimension 0
There are 2 independent parts, one for each index of `groups`. A program takes and returns all parts, laid end to end along the dimension named above; an argument that names none is the same for every part. Nothing has to cross between parts.
Inputs may be any that keep to these rules, and one draw needn't show every extreme that they name: `segment_ids`: segment ids never fall; every segment has 1 to 682 tokens, one exactly 682. `expert_ids`: A token's 8 experts differ. In the 128 rows of one device (aligned blocks of rows) no expert is named more than 80 times, and in some such block some expert is named exactly 80 times.
All inputs are finite; a program needn't handle non-finite values.
Results may differ from a plain program's by a relative error of at most 0.011.
Values may be sent and summed in bfloat16 or wider, within the bound.
A program may use at most 128 MiB of HBM per device.

v0:
```python
import jax
import jax.numpy as jnp
from jax import lax
from jax.sharding import PartitionSpec as P


def carried_in(last_seg, local_state, token_count):
    place = lax.axis_index("seq")
    blocks = lax.axis_size("seq")
    longest = token_count * blocks // 3
    reach = min(blocks - 1, max(1, (longest - 2) // token_count + 1))
    last_all = lax.all_gather(last_seg, "seq")

    def last_of(back):
        index = place - back
        return jnp.where(index >= 0, last_all[jnp.maximum(index, 0)], -1 - back)

    before = last_of(1)
    carried = None
    window = local_state
    span = 1
    covered = 0
    while covered < reach:
        shifted = lax.ppermute(
            window.astype(jnp.bfloat16), "seq", [(i, i + span) for i in range(blocks - span)]
        ).astype(jnp.float32)
        if carried is None:
            carried = shifted
        else:
            carried = carried + jnp.where(last_of(span) == before, shifted, 0.0)
        covered += span
        if covered < reach:
            window = window + jnp.where(last_of(span) == last_seg, shifted, 0.0)
        span *= 2
    return (before, carried)


def features_of(inputs, feature_map, head_count, head_dim):
    grouped = inputs.reshape(inputs.shape[0], head_count, head_dim)
    projected = jnp.einsum("thd,hdf->thf", grouped, feature_map, preferred_element_type=jnp.float32)
    return (jax.nn.elu(projected) + 1.0).astype(jnp.bfloat16)


def run_expert(rows, gate, w_gate, w_up, w_down):
    gate_pre = jnp.dot(rows, w_gate, preferred_element_type=jnp.float32)
    up_pre = jnp.dot(rows, w_up, preferred_element_type=jnp.float32)
    activated = (jax.nn.silu(gate_pre) * up_pre).astype(jnp.bfloat16)
    answer = jnp.dot(activated, w_down, preferred_element_type=jnp.float32)
    return answer * gate[:, None]


def shards(
    query_proj,
    key_proj,
    value_proj,
    segment_ids,
    feature_map,
    head_gain,
    residual,
    out_weight,
    norm_gain,
    router,
    w_gate,
    w_up,
    w_down,
    expert_ids,
):
    token_count = query_proj.shape[0]
    head_count = feature_map.shape[0]
    head_dim = feature_map.shape[1]
    query_feat = features_of(query_proj, feature_map, head_count, head_dim)
    key_feat = features_of(key_proj, feature_map, head_count, head_dim)
    values = value_proj.reshape(token_count, head_count, head_dim)
    last_seg = segment_ids[token_count - 1]
    tail_mask = (segment_ids == last_seg).astype(jnp.bfloat16)
    local_state = jnp.einsum(
        "thf,thd->hfd",
        key_feat * tail_mask[:, None, None],
        values,
        preferred_element_type=jnp.float32,
    )
    seg_before, state_before = carried_in(last_seg, local_state, token_count)
    scores = jnp.einsum("thf,shf->hts", query_feat, key_feat, preferred_element_type=jnp.float32)
    positions = lax.iota(jnp.int32, token_count)
    allowed = (positions[None, :] <= positions[:, None]) & (
        segment_ids[None, :] == segment_ids[:, None]
    )
    block_weights = jnp.where(allowed[None], scores, 0.0).astype(jnp.bfloat16)
    within = jnp.einsum("hts,shd->thd", block_weights, values, preferred_element_type=jnp.float32)
    carried = jnp.einsum(
        "thf,hfd->thd",
        query_feat,
        state_before.astype(jnp.bfloat16),
        preferred_element_type=jnp.float32,
    )
    carry_mask = (segment_ids == seg_before).astype(jnp.float32)
    mixed = within + carry_mask[:, None, None] * carried
    scale = lax.rsqrt(jnp.mean(mixed * mixed, axis=2, keepdims=True) + 1e-06)
    attn_heads = (
        (mixed * scale * head_gain.reshape(head_count, head_dim))
        .reshape(token_count, head_count * head_dim)
        .astype(jnp.bfloat16)
    )
    attn_rows = lax.all_to_all(attn_heads, "head", split_axis=0, concat_axis=1, tiled=True)
    projected = jnp.dot(
        attn_rows,
        lax.all_gather(out_weight, "head", axis=0, tiled=True),
        preferred_element_type=jnp.float32,
    )
    hidden = (residual.astype(jnp.float32) + projected).astype(jnp.bfloat16)
    hidden_f = hidden.astype(jnp.float32)
    normed = (
        hidden_f
        * lax.rsqrt(jnp.mean(hidden_f * hidden_f, axis=1, keepdims=True) + 1e-05)
        * norm_gain
    ).astype(jnp.bfloat16)
    logits = jnp.dot(normed, router, preferred_element_type=jnp.float32)
    expert_count = router.shape[1]
    expert_iota = lax.iota(jnp.int32, expert_count)
    picked = expert_ids[:, :, None] == expert_iota[None, None, :]
    chosen = jnp.sum(jnp.where(picked, logits[:, None, :], 0.0), axis=2)
    gates = jax.nn.sigmoid(chosen)
    gate_weights = gates / jnp.sum(gates, axis=1, keepdims=True)
    dense_gates = jnp.sum(jnp.where(picked, gate_weights[:, :, None], 0.0), axis=1)
    spread = ("seq", "head")
    all_rows = lax.all_gather(normed, spread, axis=0, tiled=True)
    all_gates = lax.all_gather(dense_gates, spread, axis=0, tiled=True)
    exp_dev = w_gate.shape[0]
    first = (lax.axis_index("seq") * lax.axis_size("head") + lax.axis_index("head")) * exp_dev
    partial = 0.0
    for own in range(exp_dev):
        gate = jnp.sum(jnp.where(expert_iota[None, :] == first + own, all_gates, 0.0), axis=1)
        partial = partial + run_expert(all_rows, gate, w_gate[own], w_up[own], w_down[own])
    expert_sum = lax.psum_scatter(
        partial.astype(jnp.bfloat16), spread, scatter_dimension=0, tiled=True
    )
    return (hidden, expert_sum)


def solution(mesh):
    placed = (
        P(("groups", "seq"), "head"),
        P(("groups", "seq"), "head"),
        P(("groups", "seq"), "head"),
        P(("groups", "seq")),
        P("head", None, None),
        P("head"),
        P(("groups", "seq", "head"), None),
        P("head", None),
        P(),
        P(),
        P(("seq", "head"), None, None),
        P(("seq", "head"), None, None),
        P(("seq", "head"), None, None),
        P(("groups", "seq", "head"), None),
    )
    return jax.shard_map(
        shards,
        mesh=mesh,
        in_specs=placed,
        out_specs=(P(("groups", "seq", "head"), None), P(("groups", "seq", "head"), None)),
        check_vma=False,
    )
```

profile of v0, /device:TPU:0, one launch (start us, length us, event | category | flops | bytes accessed | tf_op | source)
XLA Modules:
  0.0 290.1 jit_solution(12551976899202699490)
XLA Ops:
  7.2 0.0 copy-start
  7.2 0.0 copy-start.11
  7.2 0.0 copy-start.7
  7.2 0.0 copy-start.10
  7.2 0.0 copy-start.4
  7.2 0.0 all-gather.3.cloned.1.call-start
  7.3 0.7 all-gather.3.cloned.1.call-update
  8.0 0.0 all-gather.5.cloned.1.call-start
  8.0 0.0 copy-done.11
  8.0 0.6 dynamic-slice
  8.6 0.0 copy-done.7
  8.6 1.2 slice_dynamic-update-slice_fusion
  9.9 13.1 %all-reduce = s32[8]{0:T(128)S(1)} all-reduce(s32[8]{0:T(128)S(1)} %get-tuple-element.4), channel_id=1, replica_groups=mesh['groups'=2,'seq'=8,'head'=2] {'seq'}, use_global_device_ids=true, to_apply=%add | all-reduce | flops 8 | bytes 64
  22.9 0.6 fusion.43
  24.2 0.7 compare_convert_fusion.1
  24.9 0.0 copy-done
  24.9 0.0 copy-done.10
  24.9 1.1 fusion.12
  26.1 0.0 copy-done.4
  26.1 1.2 fusion.44
  27.3 3.4 %collective-permute-start = (bf16[8,256,128]{2,1,0:T(8,128)(2,1)}, bf16[8,256,128]{2,1,0:T(8,128)(2,1)S(1)}, u32[]{:S(2)}, u32[]{:S(2)}) collective-permute-start(bf16[8,256,128]{2,1,0:T(8,128)(2,1)} %get-tuple-element.8), channel_id=1, source_target_pairs={{0,2},{2,4},{4,6},{6,8},{8,10},{10,12},{12,14},{1,3},{3,5},{5,7},{... | collective-permute-start | bytes 1572872 | tf_op jit(solution)/shard_map/ppermute | solution.py:24
  31.4 7.9 %collective-permute-done = bf16[8,256,128]{2,1,0:T(8,128)(2,1)S(1)} collective-permute-done((bf16[8,256,128]{2,1,0:T(8,128)(2,1)}, bf16[8,256,128]{2,1,0:T(8,128)(2,1)S(1)}, u32[]{:S(2)}, u32[]{:S(2)}) %collective-permute-start) | collective-permute-done | bytes 524320 | tf_op jit(solution)/shard_map/ppermute | solution.py:24
  39.3 0.9 fusion.18
  40.2 4.4 %collective-permute-start.1 = (bf16[8,256,128]{2,1,0:T(8,128)(2,1)}, bf16[8,256,128]{2,1,0:T(8,128)(2,1)S(1)}, u32[]{:S(2)}, u32[]{:S(2)}) collective-permute-start(bf16[8,256,128]{2,1,0:T(8,128)(2,1)} %fusion.18), channel_id=1, source_target_pairs={{0,4},{2,6},{4,8},{6,10},{8,12},{10,14},{1,5},{3,7},{5,9},{7,11},{... | collective-permute-start | bytes 1572872 | tf_op jit(solution)/shard_map/ppermute | solution.py:24
  45.3 0.1 fusion.39
  45.4 2.2 fusion.9
  47.5 0.0 copy-start.2
  47.5 0.0 copy-start.9
  47.6 5.0 %collective-permute-done.1 = bf16[8,256,128]{2,1,0:T(8,128)(2,1)S(1)} collective-permute-done((bf16[8,256,128]{2,1,0:T(8,128)(2,1)}, bf16[8,256,128]{2,1,0:T(8,128)(2,1)S(1)}, u32[]{:S(2)}, u32[]{:S(2)}) %collective-permute-start.1) | collective-permute-done | bytes 524320 | tf_op jit(solution)/shard_map/ppermute | solution.py:24
  52.6 0.0 copy-done.2
  52.6 1.4 fusion.16
  54.0 0.0 copy-start.3
  54.0 2.5 multiply_reduce_fusion
  56.5 0.0 copy-done.9
  56.6 0.2 multiply_convert_fusion.2
  56.8 0.1 convert_element_type.67
  56.9 0.1 copy.47
  57.0 4.2 %all_to_all.16 = bf16[2,128,1024]{1,2,0:T(8,128)(2,1)S(1)} all-to-all(bf16[2,128,1024]{1,2,0:T(8,128)(2,1)S(1)} %copy.47), channel_id=1, replica_groups=mesh['groups'=2,'seq'=8,'head'=2] {'head'}, dimensions={0} | all-to-all | bytes 1048576 | tf_op jit(solution)/shard_map/all_to_all | solution.py:104
  61.1 0.0 all-gather.3.cloned.1.call-done
  61.1 0.0 copy-done.3
  61.1 0.0 copy-start.8
  61.1 0.0 copy-start.5
  61.1 0.0 copy-start.6
  61.2 4.8 %fusion.20 = (f32[128]{0:T(128)S(1)}, bf16[128,2048]{1,0:T(8,128)(2,1)S(1)}) fusion(bf16[128,2048]{0,1:T(8,128)(2,1)S(1)} %bitcast.71, bf16[2048,2048]{1,0:T(8,128)(2,1)} %all-gather.3.cloned.1.call-done, bf16[128,2048]{1,0:T(8,128)(2,1)S(1)} %copy-done.3), kind=kOutput, calls=%fused_computation.32 | convolution fusion | flops 1075314560 | bytes 9961984 | tf_op jit(solution)/shard_map/dot_general | solution.py:105
  66.0 0.0 copy-start.1
  66.0 0.0 copy-done.8
  66.0 1.0 fusion.22
  67.0 0.0 all-gather.5.cloned.1.call-update
  67.0 0.0 reduce-scatter.2.cloned.1.call-start
  67.1 0.0 copy-done.5
  67.1 1.3 fusion.45
  68.4 0.0 copy-done.6
  68.5 20.6 %all_gather.15 = f32[2048,16]{0,1:T(8,128)S(1)} all-gather(f32[128,16]{0,1:T(8,128)S(1)} %select_reduce_fusion.1), channel_id=1, replica_groups=mesh['groups'=2,'seq'=8,'head'=2] {'seq','head'}, dimensions={0}, use_global_device_ids=true | all-gather | bytes 139264 | tf_op jit(solution)/shard_map/all_gather | solution.py:127
  89.1 0.1 select_reduce_fusion
  89.2 51.7 %all-gather.5.cloned.1.call-done = bf16[2048,2048]{1,0:T(8,128)(2,1)} async-done(((bf16[128,2048]{1,0:T(8,128)(2,1)}), bf16[2048,2048]{1,0:T(8,128)(2,1)}) %all-gather.5.cloned.1.call-update) | async-done | bytes 8388624 | tf_op jit(solution)/shard_map/all_gather | solution.py:126
  140.9 14.4 %fusion.3 = f32[2048,1024]{1,0:T(8,128)} fusion(bf16[2048,2048]{1,0:T(8,128)(2,1)} %all-gather.5.cloned.1.call-done, bf16[1,2048,1024]{2,1,0:T(8,128)(2,1)} %param.24), kind=kOutput, calls=%fused_computation.8 | convolution fusion | flops 8589934592 | bytes 20971520 | tf_op jit(solution)/shard_map/dot_general | solution.py:45
  155.3 0.0 copy-done.1
  155.3 26.0 %multiply_convert_fusion = bf16[2048,2048]{1,0:T(8,128)(2,1)} fusion(f32[2048]{0:T(1024)S(1)} %select_reduce_fusion, f32[2048,1024]{1,0:T(8,128)} %fusion.3, bf16[2048,2048]{1,0:T(8,128)(2,1)} %all-gather.5.cloned.1.call-done, bf16[1,1024,2048]{2,1,0:T(8,128)(2,1)} %param.26, bf16[1,2048,1024]{2,1,0:T(8,128)(2,1)} %param.25), kind=kOutput, calls=%fused_computation | convolution fusion | flops 17200840704 | bytes 33562624 | tf_op jit(solution)/shard_map/dot_general | solution.py:48
  181.3 0.0 reduce-scatter.2.cloned.1.call-update
  181.3 102.2 %reduce-scatter.2.cloned.1.call-done = bf16[128,2048]{1,0:T(8,128)(2,1)} async-done(((bf16[2048,2048]{1,0:T(8,128)(2,1)}), bf16[128,2048]{1,0:T(8,128)(2,1)}) %reduce-scatter.2.cloned.1.call-update) | async-done | bytes 524304 | tf_op jit(solution)/shard_map/reduce_scatter | solution.py:134
  (8 shorter events, 0.1 us)
Async XLA Ops:
  7.2 17.7 %copy-start = (bf16[8,128,256]{2,1,0:T(8,128)(2,1)S(1)}, bf16[8,128,256]{2,1,0:T(8,128)(2,1)}, u32[]{:S(2)}) copy-start(bf16[8,128,256]{2,1,0:T(8,128)(2,1)} %param.18) | copy-start | bytes 1572868
  7.2 0.8 copy-start.11
  7.2 1.4 copy-start.7
  7.2 17.7 %copy-start.10 = (bf16[256,1024]{1,0:T(8,128)(2,1)S(1)}, bf16[256,1024]{1,0:T(8,128)(2,1)}, u32[]{:S(2)}) copy-start(bf16[256,1024]{1,0:T(8,128)(2,1)} %param.15) | copy-start | bytes 1572868
  7.2 18.8 %copy-start.4 = (bf16[256,1024]{1,0:T(8,128)(2,1)S(1)}, bf16[256,1024]{1,0:T(8,128)(2,1)}, u32[]{:S(2)}) copy-start(bf16[256,1024]{1,0:T(8,128)(2,1)} %param.16) | copy-start | bytes 1572868
  7.2 53.9 %all-gather.3.cloned.1.call-start = ((), (), s32[]{:S(2)}) async-start(), calls=%async_computation.2 | async-start | bytes 12582912 | tf_op jit(solution)/shard_map/all_gather | solution.py:107
  8.0 133.0 %all-gather.5.cloned.1.call-start = ((), (), s32[]{:S(2)}) async-start(), calls=%async_computation.3 | async-start | bytes 8912896 | tf_op jit(solution)/shard_map/all_gather | solution.py:126
  27.3 12.0 %collective-permute-start = (bf16[8,256,128]{2,1,0:T(8,128)(2,1)}, bf16[8,256,128]{2,1,0:T(8,128)(2,1)S(1)}, u32[]{:S(2)}, u32[]{:S(2)}) collective-permute-start(bf16[8,256,128]{2,1,0:T(8,128)(2,1)} %get-tuple-element.8), channel_id=1, source_target_pairs={{0,2},{2,4},{4,6},{6,8},{8,10},{10,12},{12,14},{1,3},{3,5},{5,7},{... | collective-permute-start | bytes 1572872 | tf_op jit(solution)/shard_map/ppermute | solution.py:24
  40.2 12.3 %collective-permute-start.1 = (bf16[8,256,128]{2,1,0:T(8,128)(2,1)}, bf16[8,256,128]{2,1,0:T(8,128)(2,1)S(1)}, u32[]{:S(2)}, u32[]{:S(2)}) collective-permute-start(bf16[8,256,128]{2,1,0:T(8,128)(2,1)} %fusion.18), channel_id=1, source_target_pairs={{0,4},{2,6},{4,8},{6,10},{8,12},{10,14},{1,5},{3,7},{5,9},{7,11},{... | collective-permute-start | bytes 1572872 | tf_op jit(solution)/shard_map/ppermute | solution.py:24
  47.5 5.0 %copy-start.2 = (bf16[256,8,256]{0,2,1:T(8,128)(2,1)}, bf16[256,8,256]{0,2,1:T(8,128)(2,1)S(1)}, u32[]{:S(2)}) copy-start(bf16[256,8,256]{0,2,1:T(8,128)(2,1)S(1)} %fusion.9) | copy-start | bytes 3145732
  47.5 9.0 %copy-start.9 = (f32[1024]{0:T(1024)S(1)}, f32[1024]{0:T(1024)}, u32[]{:S(2)}) copy-start(f32[1024]{0:T(1024)} %param.19) | copy-start | bytes 12292
  54.0 7.1 %copy-start.3 = (bf16[128,2048]{1,0:T(8,128)(2,1)S(1)}, bf16[128,2048]{1,0:T(8,128)(2,1)}, u32[]{:S(2)}) copy-start(bf16[128,2048]{1,0:T(8,128)(2,1)} %param.20) | copy-start | bytes 1572868
  61.1 4.9 %copy-start.8 = (f32[2048]{0:T(1024)S(1)}, f32[2048]{0:T(1024)}, u32[]{:S(2)}) copy-start(f32[2048]{0:T(1024)} %param.22) | copy-start | bytes 24580
  61.1 5.9 %copy-start.5 = (bf16[2048,16]{0,1:T(8,128)(2,1)S(1)}, bf16[2048,16]{0,1:T(8,128)(2,1)}, u32[]{:S(2)}) copy-start(bf16[2048,16]{0,1:T(8,128)(2,1)} %param.23) | copy-start | bytes 196612
  61.1 7.2 %copy-start.6 = (s32[128,8]{0,1:T(8,128)S(1)}, s32[128,8]{0,1:T(8,128)}, u32[]{:S(2)}) copy-start(s32[128,8]{0,1:T(8,128)} %param.27) | copy-start | bytes 12292
  66.0 89.4 %copy-start.1 = (bf16[128,2048]{1,0:T(8,128)(2,1)}, bf16[128,2048]{1,0:T(8,128)(2,1)S(1)}, u32[]{:S(2)}) copy-start(bf16[128,2048]{1,0:T(8,128)(2,1)S(1)} %get-tuple-element.13) | copy-start | bytes 1572868
  67.0 216.5 %reduce-scatter.2.cloned.1.call-start = ((), (), s32[]{:S(2)}) async-start(), calls=%async_computation.4 | async-start | bytes 8912896 | tf_op jit(solution)/shard_map/reduce_scatter | solution.py:134
Sparse Core Ops, SparseCore 0:
  9.6 22.5 all-gather.2
  67.1 73.7 all-gather.4
  181.5 102.0 reduce-scatter.1
where the time goes:
time: 290 us
  waiting for transfers between devices  168 us (58%)
  matrix products  54.9 us (19%)
  blocking collectives  37.9 us (13%)
  between operations  16 us (6%)
  starting transfers between devices  7.95 us (3%)
  other arithmetic  3.09 us (1%)
    reduce_scatter x1, waiting for transfers between devices, shards(): lax.psum_scatter(partial.astype(jnp.bfloat16), spread, scatter_dimension=...  102 us
    all_gather x1, waiting for transfers between devices, shards(): all_rows = lax.all_gather(normed, spread, axis=0, tiled=True)  51.7 us
    dot_general x1, matrix products, run_expert(): answer = jnp.dot(activated, w_down, preferred_element_type=jnp.float32)  26 us
    all_gather x1, blocking collectives, shards(): all_gates = lax.all_gather(dense_gates, spread, axis=0, tiled=True)  20.6 us
    dot_general x1, matrix products, run_expert(): gate_pre = jnp.dot(rows, w_gate, preferred_element_type=jnp.float32)  14.4 us
    unnamed x1, blocking collectives  13.1 us
    ppermute x2, waiting for transfers between devices, carried_in(): lax.ppermute(window.astype(jnp.bfloat16), 'seq', [(i, i + span) for i in...  12.9 us
    ppermute x2, starting transfers between devices, carried_in(): lax.ppermute(window.astype(jnp.bfloat16), 'seq', [(i, i + span) for i in...  7.83 us
  transfers between devices with their start and end apart: 5, of which 4 were waited for; matrix products, arithmetic and copies ran while one was open for 5% of the time, Pallas kernels for 0%

commit v1 on v0

--- a/solution.py
+++ b/solution.py
@@ -123,7 +123,8 @@
     gate_weights = gates / jnp.sum(gates, axis=1, keepdims=True)
     dense_gates = jnp.sum(jnp.where(picked, gate_weights[:, :, None], 0.0), axis=1)
     spread = ("seq", "head")
-    all_rows = lax.all_gather(normed, spread, axis=0, tiled=True)
+    sent = jnp.stack([normed] * lax.axis_size(spread))
+    all_rows = jnp.concatenate(lax.all_to_all(sent, spread, 0, 0), axis=0)
     all_gates = lax.all_gather(dense_gates, spread, axis=0, tiled=True)
     exp_dev = w_gate.shape[0]
     first = (lax.axis_index("seq") * lax.axis_size("head") + lax.axis_index("head")) * exp_dev

time: 290 us -> 419 us (1.44)
  blocking collectives: 37.9 us -> 183 us
  waiting for transfers between devices: 168 us -> 143 us
  starting transfers between devices: 7.95 us -> 12.8 us
  local copies, waits for them, and re-layouts: 2.73 us -> 7.02 us
    all_gather x1, blocking collectives: 20.6 us -> 166 us  [shards(): all_gates = lax.all_gather(dense_gates, spread, axis=0, tiled=True)]
    all_gather x1 -> x0, waiting for transfers between devices: 51.7 us -> none  [shards(): all_rows = lax.all_gather(normed, spread, axis=0, tiled=True)]
    reduce_scatter x1, waiting for transfers between devices: 102 us -> 130 us  [shards(): lax.psum_scatter(partial.astype(jnp.bfloat16), spread, scatter_dimension=...]
    all_to_all x0 -> x1, starting transfers between devices: none -> 4.87 us  [shards(): all_rows = jnp.concatenate(lax.all_to_all(sent, spread, 0, 0), axis=0)]
    another operation x0 -> x1, local copies, waits for them, and re-layouts: none -> 4.28 us  [shards(): sent = jnp.stack([normed] * lax.axis_size(spread))]
  transfers between devices with their start and end apart: 5 -> 5, of which waited for: 4 -> 3; matrix products, arithmetic and copies ran while one was open for 5% -> 3% of each run, Pallas kernels for 0% -> 0%
where the time goes in v1:
time: 419 us; the launch traced here: 418 us
  blocking collectives  183 us (44%)
  waiting for transfers between devices  143 us (34%)
  matrix products  53.8 us (13%)
  between operations  16.3 us (4%)
  starting transfers between devices  12.8 us (3%)
  local copies, waits for them, and re-layouts  7.02 us (2%)
    all_gather x1, blocking collectives, shards(): all_gates = lax.all_gather(dense_gates, spread, axis=0, tiled=True)  166 us
    reduce_scatter x1, waiting for transfers between devices, shards(): lax.psum_scatter(partial.astype(jnp.bfloat16), spread, scatter_dimension=...  130 us
    dot_general x1, matrix products, run_expert(): answer = jnp.dot(activated, w_down, preferred_element_type=jnp.float32)  26 us
    dot_general x1, matrix products, run_expert(): gate_pre = jnp.dot(rows, w_gate, preferred_element_type=jnp.float32)  14.4 us
    unnamed x1, blocking collectives  13.1 us
    ppermute x2, waiting for transfers between devices, carried_in(): lax.ppermute(window.astype(jnp.bfloat16), 'seq', [(i, i + span) for i in...  12.9 us
  transfers between devices with their start and end apart: 5, of which 3 were waited for; matrix products, arithmetic and copies ran while one was open for 3% of the time, Pallas kernels for 0%

profile of v1, /device:TPU:0, one launch (start us, length us, event | category | flops | bytes accessed | tf_op | source)
XLA Modules:
  0.0 418.5 jit_solution(3478359760909114407)
XLA Ops:
  7.2 0.0 copy-start
  7.2 0.0 copy-start.12
  7.2 0.0 copy-start.8
  7.2 0.0 copy-start.11
  7.2 0.0 copy-start.5
  7.2 0.0 all-gather.2.cloned.1.call-start
  7.3 0.7 all-gather.2.cloned.1.call-update
  8.0 0.0 copy-done.12
  8.0 0.6 dynamic-slice
  8.6 0.0 copy-done.8
  8.6 1.2 slice_dynamic-update-slice_fusion
  9.8 13.1 %all-reduce = s32[8]{0:T(128)S(1)} all-reduce(s32[8]{0:T(128)S(1)} %get-tuple-element.4), channel_id=1, replica_groups=mesh['groups'=2,'seq'=8,'head'=2] {'seq'}, use_global_device_ids=true, to_apply=%add | all-reduce | flops 8 | bytes 64
  22.9 0.6 fusion.43
  24.2 0.7 compare_convert_fusion.1
  24.9 0.0 copy-done
  24.9 0.0 copy-done.11
  24.9 1.1 fusion.12
  26.0 0.0 copy-done.5
  26.0 1.2 fusion.44
  27.2 3.4 collective-permute-start
  31.3 7.9 %collective-permute-done = bf16[8,256,128]{2,1,0:T(8,128)(2,1)S(1)} collective-permute-done((bf16[8,256,128]{2,1,0:T(8,128)(2,1)}, bf16[8,256,128]{2,1,0:T(8,128)(2,1)S(1)}, u32[]{:S(2)}, u32[]{:S(2)}) %collective-permute-start) | collective-permute-done | bytes 524320 | tf_op jit(solution)/shard_map/ppermute | solution.py:24
  39.3 0.9 fusion.18
  40.2 4.4 %collective-permute-start.1 = (bf16[8,256,128]{2,1,0:T(8,128)(2,1)}, bf16[8,256,128]{2,1,0:T(8,128)(2,1)S(1)}, u32[]{:S(2)}, u32[]{:S(2)}) collective-permute-start(bf16[8,256,128]{2,1,0:T(8,128)(2,1)} %fusion.18), channel_id=1, source_target_pairs={{0,4},{2,6},{4,8},{6,10},{8,12},{10,14},{1,5},{3,7},{5,9},{7,11},{... | collective-permute-start | bytes 1572872 | tf_op jit(solution)/shard_map/ppermute | solution.py:24
  45.2 0.1 fusion.39
  45.3 2.2 fusion.9
  47.5 0.0 copy-start.3
  47.5 0.0 copy-start.10
  47.5 5.0 %collective-permute-done.1 = bf16[8,256,128]{2,1,0:T(8,128)(2,1)S(1)} collective-permute-done((bf16[8,256,128]{2,1,0:T(8,128)(2,1)}, bf16[8,256,128]{2,1,0:T(8,128)(2,1)S(1)}, u32[]{:S(2)}, u32[]{:S(2)}) %collective-permute-start.1) | collective-permute-done | bytes 524320 | tf_op jit(solution)/shard_map/ppermute | solution.py:24
  52.5 0.0 copy-done.3
  52.5 1.4 fusion.16
  54.0 0.0 copy-start.4
  54.0 2.5 multiply_reduce_fusion
  56.5 0.0 copy-done.10
  56.5 0.2 multiply_convert_fusion.2
  56.7 0.1 convert_element_type.67
  56.9 0.1 copy.47
  56.9 4.2 all_to_all.21
  61.1 0.0 all-gather.2.cloned.1.call-done
  61.1 0.0 copy-done.4
  61.1 0.0 copy-start.9
  61.1 4.8 %fusion.20 = (f32[128]{0:T(128)S(1)}, bf16[128,2048]{1,0:T(8,128)(2,1)S(1)}) fusion(bf16[128,2048]{0,1:T(8,128)(2,1)S(1)} %bitcast.72, bf16[2048,2048]{1,0:T(8,128)(2,1)} %all-gather.2.cloned.1.call-done, bf16[128,2048]{1,0:T(8,128)(2,1)S(1)} %copy-done.4), kind=kOutput, calls=%fused_computation.32 | convolution fusion | flops 1075314560 | bytes 9961984 | tf_op jit(solution)/shard_map/dot_general | solution.py:105
  65.9 0.0 copy-start.2
  65.9 0.0 copy-done.9
  65.9 0.2 fusion.22
  66.1 4.3 %stack.2 = bf16[16,128,2048]{2,1,0:T(8,128)(2,1)} broadcast(bf16[128,2048]{1,0:T(8,128)(2,1)S(1)} %fusion.22), dimensions={1,2} | broadcast | bytes 8912896 | tf_op jit(solution)/shard_map/stack | solution.py:126
  70.4 0.0 copy-done.2
  70.4 0.0 copy-start.6
  70.4 0.0 copy-start.7
  70.4 4.9 %all-to-all-start.1 = ((bf16[16,128,2048]{2,1,0:T(8,128)(2,1)}), bf16[16,128,2048]{2,1,0:T(8,128)(2,1)}, u32[]{:S(2)}, u32[]{:S(2)}) async-start(bf16[16,128,2048]{2,1,0:T(8,128)(2,1)} %stack.2), calls=%async_computation.1 | async-start | bytes 16777216 | tf_op jit(solution)/shard_map/all_to_all | solution.py:127
  75.3 0.0 reduce-scatter.2.cloned.1.call-start
  75.3 0.0 copy-done.6
  75.3 0.2 fusion.45
  75.6 0.0 copy-done.7
  75.7 165.5 %all_gather.11 = f32[2048,16]{0,1:T(8,128)S(1)} all-gather(f32[128,16]{0,1:T(8,128)S(1)} %select_reduce_fusion.1), channel_id=1, replica_groups=mesh['groups'=2,'seq'=8,'head'=2] {'seq','head'}, dimensions={0}, use_global_device_ids=true | all-gather | bytes 139264 | tf_op jit(solution)/shard_map/all_gather | solution.py:128
  241.2 0.1 select_reduce_fusion
  241.3 0.0 all-to-all-done.1
  241.3 14.4 %fusion.3 = f32[2048,1024]{1,0:T(8,128)} fusion(bf16[2048,2048]{1,0:T(8,128)(2,1)} %bitcast.11, bf16[1,2048,1024]{2,1,0:T(8,128)(2,1)} %param.24), kind=kOutput, calls=%fused_computation.8 | convolution fusion | flops 8589934592 | bytes 20971520 | tf_op jit(solution)/shard_map/dot_general | solution.py:45
  255.8 26.0 %multiply_convert_fusion = bf16[2048,2048]{1,0:T(8,128)(2,1)} fusion(f32[2048]{0:T(1024)S(1)} %select_reduce_fusion, f32[2048,1024]{1,0:T(8,128)} %fusion.3, bf16[2048,2048]{1,0:T(8,128)(2,1)} %bitcast.11, bf16[1,1024,2048]{2,1,0:T(8,128)(2,1)} %param.26, bf16[1,2048,1024]{2,1,0:T(8,128)(2,1)} %param.25), kind=kOutput, calls=%fused_computation | convolution fusion | flops 17200840704 | bytes 33562624 | tf_op jit(solution)/shard_map/dot_general | solution.py:48
  281.7 0.0 copy-start.1
  281.8 0.0 reduce-scatter.2.cloned.1.call-update
  281.8 129.9 %reduce-scatter.2.cloned.1.call-done = bf16[128,2048]{1,0:T(8,128)(2,1)} async-done(((bf16[2048,2048]{1,0:T(8,128)(2,1)}), bf16[128,2048]{1,0:T(8,128)(2,1)}) %reduce-scatter.2.cloned.1.call-update) | async-done | bytes 524304 | tf_op jit(solution)/shard_map/reduce_scatter | solution.py:135
  411.6 0.0 copy-done.1
  (8 shorter events, 0.1 us)
Async XLA Ops:
  7.2 17.7 %copy-start = (bf16[8,128,256]{2,1,0:T(8,128)(2,1)S(1)}, bf16[8,128,256]{2,1,0:T(8,128)(2,1)}, u32[]{:S(2)}) copy-start(bf16[8,128,256]{2,1,0:T(8,128)(2,1)} %param.18) | copy-start | bytes 1572868
  7.2 0.8 copy-start.12
  7.2 1.4 copy-start.8
  7.2 17.7 %copy-start.11 = (bf16[256,1024]{1,0:T(8,128)(2,1)S(1)}, bf16[256,1024]{1,0:T(8,128)(2,1)}, u32[]{:S(2)}) copy-start(bf16[256,1024]{1,0:T(8,128)(2,1)} %param.15) | copy-start | bytes 1572868
  7.2 18.8 %copy-start.5 = (bf16[256,1024]{1,0:T(8,128)(2,1)S(1)}, bf16[256,1024]{1,0:T(8,128)(2,1)}, u32[]{:S(2)}) copy-start(bf16[256,1024]{1,0:T(8,128)(2,1)} %param.16) | copy-start | bytes 1572868
  7.2 53.9 %all-gather.2.cloned.1.call-start = ((), (), s32[]{:S(2)}) async-start(), calls=%async_computation.3 | async-start | bytes 12582912 | tf_op jit(solution)/shard_map/all_gather | solution.py:107
  27.2 12.0 %collective-permute-start = (bf16[8,256,128]{2,1,0:T(8,128)(2,1)}, bf16[8,256,128]{2,1,0:T(8,128)(2,1)S(1)}, u32[]{:S(2)}, u32[]{:S(2)}) collective-permute-start(bf16[8,256,128]{2,1,0:T(8,128)(2,1)} %get-tuple-element.8), channel_id=1, source_target_pairs={{0,2},{2,4},{4,6},{6,8},{8,10},{10,12},{12,14},{1,3},{3,5},{5,7},{... | collective-permute-start | bytes 1572872 | tf_op jit(solution)/shard_map/ppermute | solution.py:24
  40.2 12.3 %collective-permute-start.1 = (bf16[8,256,128]{2,1,0:T(8,128)(2,1)}, bf16[8,256,128]{2,1,0:T(8,128)(2,1)S(1)}, u32[]{:S(2)}, u32[]{:S(2)}) collective-permute-start(bf16[8,256,128]{2,1,0:T(8,128)(2,1)} %fusion.18), channel_id=1, source_target_pairs={{0,4},{2,6},{4,8},{6,10},{8,12},{10,14},{1,5},{3,7},{5,9},{7,11},{... | collective-permute-start | bytes 1572872 | tf_op jit(solution)/shard_map/ppermute | solution.py:24
  47.5 5.0 %copy-start.3 = (bf16[256,8,256]{0,2,1:T(8,128)(2,1)}, bf16[256,8,256]{0,2,1:T(8,128)(2,1)S(1)}, u32[]{:S(2)}) copy-start(bf16[256,8,256]{0,2,1:T(8,128)(2,1)S(1)} %fusion.9) | copy-start | bytes 3145732
  47.5 9.0 %copy-start.10 = (f32[1024]{0:T(1024)S(1)}, f32[1024]{0:T(1024)}, u32[]{:S(2)}) copy-start(f32[1024]{0:T(1024)} %param.19) | copy-start | bytes 12292
  54.0 7.1 %copy-start.4 = (bf16[128,2048]{1,0:T(8,128)(2,1)S(1)}, bf16[128,2048]{1,0:T(8,128)(2,1)}, u32[]{:S(2)}) copy-start(bf16[128,2048]{1,0:T(8,128)(2,1)} %param.20) | copy-start | bytes 1572868
  61.1 4.8 %copy-start.9 = (f32[2048]{0:T(1024)S(1)}, f32[2048]{0:T(1024)}, u32[]{:S(2)}) copy-start(f32[2048]{0:T(1024)} %param.22) | copy-start | bytes 24580
  65.9 4.5 %copy-start.2 = (bf16[128,2048]{1,0:T(8,128)(2,1)}, bf16[128,2048]{1,0:T(8,128)(2,1)S(1)}, u32[]{:S(2)}) copy-start(bf16[128,2048]{1,0:T(8,128)(2,1)S(1)} %get-tuple-element.13) | copy-start | bytes 1572868
  70.4 5.0 %copy-start.6 = (bf16[2048,16]{0,1:T(8,128)(2,1)S(1)}, bf16[2048,16]{0,1:T(8,128)(2,1)}, u32[]{:S(2)}) copy-start(bf16[2048,16]{0,1:T(8,128)(2,1)} %param.23) | copy-start | bytes 196612
  70.4 5.2 %copy-start.7 = (s32[128,8]{0,1:T(8,128)S(1)}, s32[128,8]{0,1:T(8,128)}, u32[]{:S(2)}) copy-start(s32[128,8]{0,1:T(8,128)} %param.27) | copy-start | bytes 12292
  70.4 171.0 %all-to-all-start.1 = ((bf16[16,128,2048]{2,1,0:T(8,128)(2,1)}), bf16[16,128,2048]{2,1,0:T(8,128)(2,1)}, u32[]{:S(2)}, u32[]{:S(2)}) async-start(bf16[16,128,2048]{2,1,0:T(8,128)(2,1)} %stack.2), calls=%async_computation.1 | async-start | bytes 16777216 | tf_op jit(solution)/shard_map/all_to_all | solution.py:127
  75.3 336.4 %reduce-scatter.2.cloned.1.call-start = ((), (), s32[]{:S(2)}) async-start(), calls=%async_computation.4 | async-start | bytes 8912896 | tf_op jit(solution)/shard_map/reduce_scatter | solution.py:135
  281.7 129.9 %copy-start.1 = (bf16[8,128,256]{2,1,0:T(8,128)(2,1)S(1)}, bf16[8,128,256]{2,1,0:T(8,128)(2,1)}, u32[]{:S(2)}) copy-start(bf16[8,128,256]{2,1,0:T(8,128)(2,1)} %param.18) | copy-start | bytes 1572868
Sparse Core Ops, SparseCore 0:
  9.6 22.5 all-gather.1
  281.9 129.6 reduce-scatter.1
